TPU v7x, 512 devices: a whole 4x8x8 slice. The times are simulated.
512 devices in a mesh: row: 32 (over y, x_hi, core), col: 16 (over x_lo, z).
Axes of the slice: x: 4 (x_hi: 2, x_lo: 2; x = x_hi * 2 + x_lo), y: 8, z: 8, core: 2. Of those that a mesh axis runs over, the one named last changes fastest.
Arguments:
- tile_blocks: bfloat16 [12288, 128, 128], P(('row', 'col')), may hold values from -0.21875 to 0.21875
- tile_rows: int32 [12288], P(('row', 'col')), may hold values from 0 to 4095, as said below
- tile_cols: int32 [12288], P(('row', 'col')), may hold values from 0 to 4095, as said below
- trial_vectors: bfloat16 [4, 524288], P(None, ('col', 'row')), may hold values from -6 to 6
- basis_old: float32 [44, 524288], P(None, ('col', 'row'))
- image_old: float32 [44, 524288], P(None, ('col', 'row'))
Outputs:
- projected: float32 [48, 48], replicated
- basis_new: float32 [48, 524288], P(None, ('col', 'row'))
- image_new: float32 [48, 524288], P(None, ('col', 'row'))
Inputs may be any that keep to these rules, and one draw needn't show every extreme that they name: `tile_rows`: the 24 tiles of each device with index r on row have block rows b for which (b // 8) % 32 equals r. `tile_cols`: the 24 tiles of each device with index c on col have block columns from c * 256 to (c + 1) * 256 - 1.
All inputs are finite; a program needn't handle non-finite values.
Results may differ from a plain program's by a relative error of at most 0.0003.
Values may be sent and summed in bfloat16 or wider, within the bound.
A program may use at most 64 MiB of HBM per device.

v0:
```python
import jax
import jax.numpy as jnp
from jax import lax
from jax.sharding import PartitionSpec as P


def rows_product(left, right):
    return lax.dot_general(left, right, (((1,), (1,)), ((), ())), precision=lax.Precision.HIGHEST)


def place_blocks(local_index, block_count, products):
    onehot = (local_index[None, :] == jnp.arange(block_count, dtype=jnp.int32)[:, None]).astype(
        jnp.float32
    )
    flat = products.reshape(products.shape[0], -1)
    placed = jnp.dot(onehot, flat, precision=lax.Precision.HIGHEST)
    return placed.reshape(block_count, products.shape[1], products.shape[2])


def local(tile_blocks, tile_rows, tile_cols, trial_vectors, basis_old, image_old):
    tile_size = tile_blocks.shape[1]
    piece_width = trial_vectors.shape[1]
    vec_count = trial_vectors.shape[0]
    blocks_dev = piece_width // tile_size
    n_row = lax.axis_size("row")
    n_col = lax.axis_size("col")
    row_blocks = blocks_dev * n_col
    col_blocks = blocks_dev * n_row
    row_index = lax.axis_index("row")
    col_index = lax.axis_index("col")
    all_rows = float(piece_width * n_row * n_col)
    gathered = lax.all_gather(trial_vectors, ("row", "col"), axis=1, tiled=True)
    grid = gathered.reshape(vec_count, n_row, n_col, piece_width)
    col_vectors = lax.dynamic_index_in_dim(grid, col_index, 2, keepdims=False).reshape(
        vec_count, -1
    )
    row_vectors = lax.dynamic_index_in_dim(grid, row_index, 1, keepdims=False).reshape(
        vec_count, -1
    )
    local_rows = tile_rows // blocks_dev // n_row * blocks_dev + tile_rows % blocks_dev
    local_cols = tile_cols - col_index * col_blocks
    picked_cols = jnp.take(
        col_vectors.reshape(vec_count, col_blocks, tile_size), local_cols, axis=1
    )
    forward = jnp.einsum(
        "ktb,tab->tka", picked_cols, tile_blocks, preferred_element_type=jnp.float32
    )
    picked_rows = jnp.take(
        row_vectors.reshape(vec_count, row_blocks, tile_size), local_rows, axis=1
    )
    backward = jnp.einsum(
        "kta,tab->tkb", picked_rows, tile_blocks, preferred_element_type=jnp.float32
    )
    row_partial = place_blocks(local_rows, row_blocks, forward)
    col_partial = place_blocks(local_cols, col_blocks, backward)
    col_share = lax.psum_scatter(col_partial, "row", scatter_dimension=0, tiled=True)
    row_total = lax.psum(row_partial, "col")
    own_rows = lax.dynamic_slice_in_dim(row_total, col_index * blocks_dev, blocks_dev, 0)
    new_image = (own_rows + col_share).transpose(1, 0, 2).reshape(vec_count, piece_width)
    trial_wide = trial_vectors.astype(jnp.float32)
    basis_all = jnp.concatenate([basis_old, trial_wide], axis=0)
    images_all = jnp.concatenate([image_old, new_image], axis=0)
    correlation, coupling = lax.psum(
        (rows_product(basis_all, basis_all), rows_product(basis_all, images_all)), ("row", "col")
    )
    correlation = correlation / all_rows
    coupling = coupling / all_rows
    factor = jnp.linalg.cholesky(correlation)

    def solve_lower(matrix):
        return lax.linalg.triangular_solve(factor, matrix, left_side=True, lower=True)

    half_done = solve_lower(coupling)
    projected = solve_lower(half_done.T).T
    return (projected, solve_lower(basis_all), solve_lower(images_all))


def solution(mesh):
    in_specs = (
        P(("row", "col"), None, None),
        P(("row", "col")),
        P(("row", "col")),
        P(None, ("col", "row")),
        P(None, ("col", "row")),
        P(None, ("col", "row")),
    )
    out_specs = (P(), P(None, ("col", "row")), P(None, ("col", "row")))
    return jax.shard_map(local, mesh=mesh, in_specs=in_specs, out_specs=out_specs, check_vma=False)
```

profile of v0, /device:TPU:1, one launch (start us, length us, event | category | flops | bytes accessed | tf_op | source)
XLA Modules:
  0.0 1796.1 jit_solution(15084369518175985899)
XLA Ops:
  7.2 0.0 copy-start
  7.2 0.0 all-gather.2.cloned.1.call-start
  7.2 0.7 all-gather.2.cloned.1.call-update
  7.9 0.0 all-reduce.3.cloned.1.call-start
  8.0 0.7 compare_and_fusion
  8.7 1393.4 %all-gather.2.cloned.1.call-done = bf16[4,524288]{1,0:T(4,128)(2,1)} async-done(((bf16[4,1024]{1,0:T(4,128)(2,1)}), bf16[4,524288]{1,0:T(4,128)(2,1)}) %all-gather.2.cloned.1.call-update) | async-done | bytes 4194320 | tf_op jit(solution)/shard_map/all_gather | solution.py:32
  1402.1 3.6 copy.35
  1405.7 0.0 copy-start.1
  1405.7 0.0 copy-start.4
  1405.7 0.0 copy-start.2
  1405.7 0.0 copy-start.3
  1405.7 1.9 copy-done.1
  1407.6 1.5 dynamic-slice_reduce_fusion
  1409.2 0.1 reshape_reshape.6
  1409.3 0.2 copy.22
  1409.5 0.6 gather_fusion
  1410.1 0.0 copy-done
  1410.1 0.5 fusion.13
  1410.6 1.1 fusion.7
  1411.7 0.0 all-reduce.3.cloned.1.call-update
  1411.8 0.0 reduce-scatter.2.cloned.1.call-start
  1411.8 0.9 dynamic-slice_bitcast_fusion
  1412.7 0.1 reshape_reshape.7
  1412.8 0.1 copy.25
  1412.9 0.6 gather_fusion.1
  1413.5 0.4 fusion.11
  1413.9 1.3 fusion.4
  1415.2 0.0 reduce-scatter.2.cloned.1.call-update
  1415.2 0.0 copy-done.4
  1415.2 0.0 copy-done.2
  1415.2 0.3 fusion.3
  1415.5 128.8 %all-reduce.3.cloned.1.call-done = f32[128,4,128]{2,0,1:T(8,128)} async-done(((f32[128,4,128]{2,0,1:T(8,128)}), f32[128,4,128]{2,0,1:T(8,128)}) %all-reduce.3.cloned.1.call-update) | async-done | bytes 262160 | tf_op jit(solution)/shard_map/psum | solution.py:57
  1544.3 129.5 %reduce-scatter.2.cloned.1.call-done = f32[8,4,128]{2,0,1:T(8,128)} async-done(((f32[256,4,128]{2,0,1:T(8,128)}), f32[8,4,128]{2,0,1:T(8,128)}) %reduce-scatter.2.cloned.1.call-update) | async-done | bytes 16400 | tf_op jit(solution)/shard_map/reduce_scatter | solution.py:56
  1673.8 0.7 add_bitcast_fusion
  1674.5 0.0 copy-done.3
  1674.6 0.3 fusion.1
  1674.9 102.0 %all-reduce = (f32[48,48]{0,1:T(8,128)S(1)}, f32[48,48]{0,1:T(8,128)S(1)}) all-reduce(f32[48,48]{0,1:T(8,128)S(1)} %fusion.3, f32[48,48]{0,1:T(8,128)S(1)} %fusion.1), channel_id=1, replica_groups=mesh['row'=32,'col'=16] {'row','col'}, use_global_device_ids=true, to_apply=%region_0.1 | all-reduce | flops 4608 | bytes 36864 | tf_op jit(solution)/shard_map/psum | solution.py:63
  1776.9 0.1 copy.20
  1777.0 4.4 cholesky.18
  1781.4 0.6 compare_reduce_fusion
  1782.0 0.7 fusion.10
  1782.7 3.7 custom-call.12
  1786.4 1.1 fusion
  1787.4 1.0 fusion.2
  1788.5 0.2 convolution_bitcast_fusion.1
  1788.7 0.2 convolution_bitcast_fusion
  1788.9 0.7 copy.28
  (9 shorter events, 0.1 us)
Async XLA Ops:
  7.2 1402.9 %copy-start = (bf16[24,128,128]{2,1,0:T(8,128)(2,1)S(1)}, bf16[24,128,128]{2,1,0:T(8,128)(2,1)}, u32[]{:S(2)}) copy-start(bf16[24,128,128]{2,1,0:T(8,128)(2,1)} %param.10) | copy-start | bytes 2359300
  7.2 1394.9 %all-gather.2.cloned.1.call-start = ((), (), s32[]{:S(2)}) async-start(), calls=%async_computation.1 | async-start | bytes 4202496 | tf_op jit(solution)/shard_map/all_gather | solution.py:32
  7.9 1536.4 %all-reduce.3.cloned.1.call-start = ((), (), s32[]{:S(2)}) async-start(), calls=%async_computation.2 | async-start | bytes 524288 | tf_op jit(solution)/shard_map/psum | solution.py:57
  1405.7 1.9 copy-start.1
  1405.7 9.5 copy-start.4
  1405.7 9.5 copy-start.2
  1405.7 268.8 %copy-start.3 = (f32[44,1024]{1,0:T(8,128)S(1)}, f32[44,1024]{1,0:T(8,128)}, u32[]{:S(2)}) copy-start(f32[44,1024]{1,0:T(8,128)} %param.15) | copy-start | bytes 540676
  1411.8 262.0 %reduce-scatter.2.cloned.1.call-start = ((), (), s32[]{:S(2)}) async-start(), calls=%async_computation.3 | async-start | bytes 540672 | tf_op jit(solution)/shard_map/reduce_scatter | solution.py:56
Sparse Core Ops, SparseCore 0:
  10.2 1391.8 all-gather.1
  1411.9 132.4 all-reduce.2
  1549.6 124.1 reduce-scatter.1
where the time goes:
time: 1800 us
  waiting for transfers between devices  1650 us (92%)
  blocking collectives  102 us (6%)
    all_gather x1, waiting for transfers between devices, local(): gathered = lax.all_gather(trial_vectors, ('row', 'col'), axis=1, tiled=True)  1390 us
    reduce_scatter x1, waiting for transfers between devices, local(): lax.psum_scatter(col_partial, 'row', scatter_dimension=0, tiled=True)  129 us
    psum x1, waiting for transfers between devices, local(): row_total = lax.psum(row_partial, 'col')  129 us
    psum x1, blocking collectives, local(): lax.psum((rows_product(basis_all, basis_all), rows_product(basis_all, ima...  102 us
  transfers between devices with their start and end apart: 3, of which 3 were waited for; matrix products, arithmetic and copies ran while one was open for 0% of the time, Pallas kernels for 0%

commit v1 on v0

--- a/solution.py
+++ b/solution.py
@@ -61,7 +61,8 @@
     basis_all = jnp.concatenate([basis_old, trial_wide], axis=0)
     images_all = jnp.concatenate([image_old, new_image], axis=0)
     correlation, coupling = lax.psum(
-        (rows_product(basis_all, basis_all), rows_product(basis_all, images_all)), ("row", "col")
+        lax.psum((rows_product(basis_all, basis_all), rows_product(basis_all, images_all)), "row"),
+        "col",
     )
     correlation = correlation / all_rows
     coupling = coupling / all_rows

time: 1800 us -> 1890 us (1.050)
  blocking collectives: 102 us -> 178 us
    psum x0 -> x1, blocking collectives: none -> 49.7 us  [local(): lax.psum(lax.psum((rows_product(basis_all, basis_all), rows_product(basis...]
    psum x1, blocking collectives: 102 us -> 129 us  [local(): lax.psum((rows_product(basis_all, basis_all), rows_product(basis_all, ima...]
where the time goes in v1:
time: 1890 us; the launch traced here: 1870 us
  waiting for transfers between devices  1650 us (87%)
  blocking collectives  178 us (9%)
    all_gather x1, waiting for transfers between devices, local(): gathered = lax.all_gather(trial_vectors, ('row', 'col'), axis=1, tiled=True)  1390 us
    reduce_scatter x1, waiting for transfers between devices, local(): lax.psum_scatter(col_partial, 'row', scatter_dimension=0, tiled=True)  129 us
    psum x1, waiting for transfers between devices, local(): row_total = lax.psum(row_partial, 'col')  129 us
    psum x1, blocking collectives, local(): lax.psum((rows_product(basis_all, basis_all), rows_product(basis_all, ima...  129 us
    psum x1, blocking collectives, local(): lax.psum(lax.psum((rows_product(basis_all, basis_all), rows_product(basis...  49.7 us
  transfers between devices with their start and end apart: 3, of which 3 were waited for; matrix products, arithmetic and copies ran while one was open for 0% of the time, Pallas kernels for 0%

profile of v1, /device:TPU:1, one launch (start us, length us, event | category | flops | bytes accessed | tf_op | source)
XLA Modules:
  0.0 1872.5 jit_solution(8834152733532860029)
XLA Ops:
  7.2 0.0 copy-start
  7.2 0.0 all-gather.2.cloned.1.call-start
  7.2 0.7 all-gather.2.cloned.1.call-update
  7.9 0.0 all-reduce.4.cloned.1.call-start
  8.0 0.7 compare_and_fusion
  8.7 1393.4 %all-gather.2.cloned.1.call-done = bf16[4,524288]{1,0:T(4,128)(2,1)} async-done(((bf16[4,1024]{1,0:T(4,128)(2,1)}), bf16[4,524288]{1,0:T(4,128)(2,1)}) %all-gather.2.cloned.1.call-update) | async-done | bytes 4194320 | tf_op jit(solution)/shard_map/all_gather | solution.py:32
  1402.1 3.6 copy.35
  1405.7 0.0 copy-start.1
  1405.7 0.0 copy-start.4
  1405.7 0.0 copy-start.2
  1405.7 0.0 copy-start.3
  1405.7 1.9 copy-done.1
  1407.6 1.5 dynamic-slice_reduce_fusion
  1409.2 0.1 reshape_reshape.6
  1409.3 0.2 copy.22
  1409.5 0.6 gather_fusion
  1410.1 0.0 copy-done
  1410.1 0.5 fusion.13
  1410.6 1.1 fusion.7
  1411.7 0.0 all-reduce.4.cloned.1.call-update
  1411.8 0.0 reduce-scatter.2.cloned.1.call-start
  1411.8 0.9 dynamic-slice_bitcast_fusion
  1412.7 0.1 reshape_reshape.7
  1412.8 0.1 copy.25
  1412.9 0.6 gather_fusion.1
  1413.5 0.4 fusion.11
  1413.9 1.3 fusion.4
  1415.2 0.0 reduce-scatter.2.cloned.1.call-update
  1415.2 0.0 copy-done.4
  1415.2 0.0 copy-done.2
  1415.2 0.3 fusion.3
  1415.5 128.8 %all-reduce.4.cloned.1.call-done = f32[128,4,128]{2,0,1:T(8,128)} async-done(((f32[128,4,128]{2,0,1:T(8,128)}), f32[128,4,128]{2,0,1:T(8,128)}) %all-reduce.4.cloned.1.call-update) | async-done | bytes 262160 | tf_op jit(solution)/shard_map/psum | solution.py:57
  1544.3 129.5 %reduce-scatter.2.cloned.1.call-done = f32[8,4,128]{2,0,1:T(8,128)} async-done(((f32[256,4,128]{2,0,1:T(8,128)}), f32[8,4,128]{2,0,1:T(8,128)}) %reduce-scatter.2.cloned.1.call-update) | async-done | bytes 16400 | tf_op jit(solution)/shard_map/reduce_scatter | solution.py:56
  1673.8 0.7 add_bitcast_fusion
  1674.5 0.0 copy-done.3
  1674.6 0.3 fusion.1
  1674.9 128.7 %all-reduce = (f32[48,48]{0,1:T(8,128)S(1)}, f32[48,48]{0,1:T(8,128)S(1)}) all-reduce(f32[48,48]{0,1:T(8,128)S(1)} %fusion.3, f32[48,48]{0,1:T(8,128)S(1)} %fusion.1), channel_id=1, replica_groups=mesh['row'=32,'col'=16] {'row'}, use_global_device_ids=true, to_apply=%region_0.1 | all-reduce | flops 4608 | bytes 36864 | tf_op jit(solution)/shard_map/psum | solution.py:64
  1803.5 49.7 %all-reduce.1 = (f32[48,48]{0,1:T(8,128)S(1)}, f32[48,48]{0,1:T(8,128)S(1)}) all-reduce(f32[48,48]{0,1:T(8,128)S(1)} %get-tuple-element.14, f32[48,48]{0,1:T(8,128)S(1)} %get-tuple-element.15), channel_id=1, replica_groups=mesh['row'=32,'col'=16] {'col'}, use_global_device_ids=true, to_apply=%region_1.2 | all-reduce | flops 4608 | bytes 36864 | tf_op jit(solution)/shard_map/psum | solution.py:63
  1853.2 0.1 copy.20
  1853.3 4.4 cholesky.18
  1857.8 0.6 compare_reduce_fusion
  1858.4 0.7 fusion.10
  1859.1 3.7 custom-call.12
  1862.7 1.1 fusion
  1863.8 1.0 fusion.2
  1864.8 0.2 convolution_bitcast_fusion.1
  1865.0 0.2 convolution_bitcast_fusion
  1865.3 0.7 copy.28
  (9 shorter events, 0.1 us)
Async XLA Ops:
  7.2 1402.9 %copy-start = (bf16[24,128,128]{2,1,0:T(8,128)(2,1)S(1)}, bf16[24,128,128]{2,1,0:T(8,128)(2,1)}, u32[]{:S(2)}) copy-start(bf16[24,128,128]{2,1,0:T(8,128)(2,1)} %param.10) | copy-start | bytes 2359300
  7.2 1394.9 %all-gather.2.cloned.1.call-start = ((), (), s32[]{:S(2)}) async-start(), calls=%async_computation.1 | async-start | bytes 4202496 | tf_op jit(solution)/shard_map/all_gather | solution.py:32
  7.9 1536.4 %all-reduce.4.cloned.1.call-start = ((), (), s32[]{:S(2)}) async-start(), calls=%async_computation.2 | async-start | bytes 524288 | tf_op jit(solution)/shard_map/psum | solution.py:57
  1405.7 1.9 copy-start.1
  1405.7 9.5 copy-start.4
  1405.7 9.5 copy-start.2
  1405.7 268.8 %copy-start.3 = (f32[44,1024]{1,0:T(8,128)S(1)}, f32[44,1024]{1,0:T(8,128)}, u32[]{:S(2)}) copy-start(f32[44,1024]{1,0:T(8,128)} %param.15) | copy-start | bytes 540676
  1411.8 262.0 %reduce-scatter.2.cloned.1.call-start = ((), (), s32[]{:S(2)}) async-start(), calls=%async_computation.3 | async-start | bytes 540672 | tf_op jit(solution)/shard_map/reduce_scatter | solution.py:56
Sparse Core Ops, SparseCore 0:
  10.2 1391.8 all-gather.1
  1411.9 132.4 all-reduce.3
  1549.6 124.1 reduce-scatter.1
